TPU v7x, 512 devices: a whole 4x4x16 slice. The times are simulated.
512 devices in a mesh: tile: 64 (over z, y_lo, core), head: 8 (over x, y_hi).
Axes of the slice: x: 4, y: 4 (y_hi: 2, y_lo: 2; y = y_hi * 2 + y_lo), z: 16, core: 2. Of those that a mesh axis runs over, the one named last changes fastest.
Arguments:
- query_rows: bfloat16 [24576, 5120], P('tile', 'head'), may hold values from -60 to 60
- key_rows: bfloat16 [24576, 5120], P('tile', 'head'), may hold values from -60 to 60
- value_rows: bfloat16 [24576, 5120], P('tile', 'head'), may hold values from -6 to 6
- gain_q: float32 [5120], P('head'), may hold values from 0.1 to 1.9
- gain_k: float32 [5120], P('head'), may hold values from 0.1 to 1.9
- mem_keys: bfloat16 [1024, 8, 5120], P('tile', None, 'head'), may hold values from -6 to 6
- mem_values: bfloat16 [1024, 8, 5120], P('tile', None, 'head'), may hold values from -6 to 6
- tile_len: int32 [64], P('tile'), may hold values from 1 to 384, 18432 in all
- session: int32 [64], P('tile'), may hold values from 0 to 5, never falling along the last dimension, each value on 1 to 17 neighbouring positions
- req_owner: int32 [4096, 1], P('tile'), may hold values from 0 to 63; in each aligned block of 64 rows (0 to 63, 64 to 127, ...) at most 2 rows name the same one
- requested_block_index: int32 [4096], P('tile'), may hold values from 0 to 15
Outputs:
- attended: bfloat16 [24576, 5120], P('tile', 'head')
Inputs may be any that keep to these rules, and one draw needn't show every extreme that they name: Each session's tiles stand in a row, the session numbers never falling along tiles; a session has 1 to 17 tiles. `req_owner`: among the 64 requests of one tile at most 2 name the same owner, and exactly 2 do for some owner and tile.
All inputs are finite; a program needn't handle non-finite values. No bound on the sum of `tile_len` on one device may be relied on, other than what follows from the above.
Results may differ from a plain program's by a relative error of at most 0.011.
Values may be sent and summed in bfloat16 or wider, within the bound.
A program may use at most 64 MiB of HBM per device.

v0:
```python
import jax
import jax.numpy as jnp
from jax import lax
from jax.sharding import PartitionSpec as P

HEAD_DIM = 128
WIDTH = 5120
EDGE = 64


EPSILON = 1e-06


def passed_along(value, axis, steps):
    count = lax.axis_size(axis)
    first, last = (max(0, -steps), min(count, count - steps))
    return lax.ppermute(value, axis, [(source, source + steps) for source in range(first, last)])


def row_squares(raw_rows):
    rows32 = raw_rows.astype(jnp.float32)
    return jnp.sum(rows32 * rows32, axis=1)


def normalize(raw_rows, totals, gain):
    rows32 = raw_rows.astype(jnp.float32)
    factor = lax.rsqrt(totals / WIDTH + EPSILON)
    return (rows32 * factor[:, None] * gain).astype(jnp.bfloat16)


def per_device(
    query_rows,
    key_rows,
    value_rows,
    gain_q,
    gain_k,
    mem_keys,
    mem_values,
    tile_len,
    session,
    req_owner,
    requested_block_index,
):
    spatial_tile_count = lax.axis_size("tile")
    capacity, tile_local_width = query_rows.shape
    my_length = tile_len[0]
    own_label = (session[0] + 1).astype(jnp.bfloat16)
    edge_index = jnp.arange(EDGE, dtype=jnp.int32)
    tail_labels = jnp.where(edge_index >= EDGE - my_length, own_label, jnp.bfloat16(0))
    front_labels = jnp.where(edge_index < my_length, own_label, jnp.bfloat16(0))
    totals_q, totals_k = lax.psum((row_squares(query_rows), row_squares(key_rows)), "head")
    query_norm = normalize(query_rows, totals_q, gain_q)
    key_norm = normalize(key_rows, totals_k, gain_k)
    blank = jnp.zeros((EDGE, tile_local_width), jnp.bfloat16)
    tail_keys = lax.dynamic_slice_in_dim(jnp.concatenate([blank, key_norm], 0), my_length, EDGE, 0)
    tail_values = lax.dynamic_slice_in_dim(
        jnp.concatenate([blank, value_rows], 0), my_length, EDGE, 0
    )
    from_left = passed_along((tail_keys, tail_values, tail_labels), "tile", 1)
    from_right = passed_along((key_norm[:EDGE], value_rows[:EDGE], front_labels), "tile", -1)
    from_left, from_right = (from_left, from_right)
    left_keys = from_left[0]
    right_keys = from_right[0]
    retrieved_count = requested_block_index.shape[0]
    owners = req_owner[:, 0]
    rows_per_block = mem_keys.shape[1]
    memory_slot_count = max(2, 2 * retrieved_count // spatial_tile_count)
    request_sequence = jnp.arange(retrieved_count, dtype=jnp.int32)
    earlier_same = (owners[:, None] == owners[None, :]) & (
        request_sequence[None, :] < request_sequence[:, None]
    )
    owner_ranks = jnp.sum(earlier_same.astype(jnp.int32), axis=1)
    slot_index = owners * memory_slot_count + owner_ranks
    slot_onehot = (
        slot_index[:, None]
        == jnp.arange(spatial_tile_count * memory_slot_count, dtype=jnp.int32)[None, :]
    ).astype(jnp.int32)
    wanted = (jnp.sum(slot_onehot * (requested_block_index + 1)[:, None], axis=0) - 1).reshape(
        spatial_tile_count, memory_slot_count
    )
    asked = lax.all_to_all(wanted, "tile", split_axis=0, concat_axis=0, tiled=True)
    present = (asked >= 0)[:, :, None, None]
    safe_index = jnp.maximum(asked, 0)
    picked_keys = jnp.where(present, jnp.take(mem_keys, safe_index, axis=0), jnp.bfloat16(0))
    picked_values = jnp.where(present, jnp.take(mem_values, safe_index, axis=0), jnp.bfloat16(0))
    got_keys = lax.all_to_all(picked_keys, "tile", split_axis=0, concat_axis=0, tiled=True)
    got_values = lax.all_to_all(picked_values, "tile", split_axis=0, concat_axis=0, tiled=True)
    flat_keys = got_keys.reshape(
        spatial_tile_count * memory_slot_count, rows_per_block, tile_local_width
    )
    flat_values = got_values.reshape(
        spatial_tile_count * memory_slot_count, rows_per_block, tile_local_width
    )
    memory_keys = jnp.take(flat_keys, slot_index, axis=0).reshape(
        retrieved_count * rows_per_block, tile_local_width
    )
    memory_values = jnp.take(flat_values, slot_index, axis=0).reshape(
        retrieved_count * rows_per_block, tile_local_width
    )
    live_rows = jnp.arange(capacity, dtype=jnp.int32) < my_length
    all_keys = jnp.concatenate([key_norm, left_keys, right_keys, memory_keys], 0)
    all_values = jnp.concatenate([value_rows, from_left[1], from_right[1], memory_values], 0)
    visible = jnp.concatenate(
        [
            live_rows,
            from_left[2] == own_label,
            from_right[2] == own_label,
            jnp.ones((retrieved_count * rows_per_block,), bool),
        ],
        0,
    )
    heads_here = tile_local_width // HEAD_DIM
    score_scale = 1.0 / HEAD_DIM**0.5

    def one_head(head_number):
        first = head_number * HEAD_DIM
        head_query = lax.dynamic_slice_in_dim(query_norm, first, HEAD_DIM, 1)
        head_keys = lax.dynamic_slice_in_dim(all_keys, first, HEAD_DIM, 1)
        head_values = lax.dynamic_slice_in_dim(all_values, first, HEAD_DIM, 1)
        scores = (
            lax.dot_general(
                head_query, head_keys, (((1,), (1,)), ((), ())), preferred_element_type=jnp.float32
            )
            * score_scale
        )
        scores = jnp.where(visible[None, :], scores, jnp.float32(-1e30))
        top = jnp.max(scores, axis=1, keepdims=True)
        expo = jnp.exp(scores - top)
        weights = (expo / jnp.sum(expo, axis=1, keepdims=True)).astype(jnp.bfloat16)
        return jnp.dot(weights, head_values, preferred_element_type=jnp.float32)

    outputs = lax.map(one_head, jnp.arange(heads_here, dtype=jnp.int32))
    attended = jnp.transpose(outputs, (1, 0, 2)).reshape(capacity, tile_local_width)
    return jnp.where(live_rows[:, None], attended, jnp.float32(0.0)).astype(jnp.bfloat16)


def solution(mesh):
    in_specs = (
        P("tile", "head"),
        P("tile", "head"),
        P("tile", "head"),
        P("head"),
        P("head"),
        P("tile", None, "head"),
        P("tile", None, "head"),
        P("tile"),
        P("tile"),
        P("tile", None),
        P("tile"),
    )
    out_specs = P("tile", "head")
    return jax.shard_map(
        per_device, mesh=mesh, in_specs=in_specs, out_specs=out_specs, check_vma=False
    )
```

profile of v0, /device:TPU:1, one launch (start us, length us, event | category | flops | bytes accessed | tf_op | source)
XLA Modules:
  0.0 200.4 jit_solution(6113152422239226431)
XLA Ops:
  2.5 31.2 %all_to_all.16 = s32[64,1,2]{2,1,0:T(1,128)S(1)} all-to-all(s32[64,1,2]{2,1,0:T(1,128)S(1)} %bitcast.52), channel_id=1, replica_groups=mesh['tile'=64,'head'=8] {'tile'}, dimensions={0} | all-to-all | bytes 1024 | tf_op jit(solution)/shard_map/all_to_all | solution.py:81
  36.0 1.5 select_select_fusion
  37.5 68.8 %all_to_all.17 = bf16[64,2,8,640]{3,2,1,0:T(8,128)(2,1)S(1)} all-to-all(bf16[64,2,8,640]{3,2,1,0:T(8,128)(2,1)S(1)} %get-tuple-element.70), channel_id=1, replica_groups=mesh['tile'=64,'head'=8] {'tile'}, dimensions={0} | all-to-all | bytes 2621440 | tf_op jit(solution)/shard_map/all_to_all | solution.py:86
  106.3 7.3 %all-to-all-start.2 = ((bf16[64,2,8,640]{3,2,1,0:T(8,128)(2,1)}), bf16[64,2,8,640]{3,2,1,0:T(8,128)(2,1)S(1)}, u32[]{:S(2)}, u32[]{:S(2)}) async-start(bf16[64,2,8,640]{3,2,1,0:T(8,128)(2,1)} %get-tuple-element.69), calls=%async_computation.2 | async-start | bytes 2621440 | tf_op jit(solution)/shard_map/all_to_all | solution.py:87
  114.2 1.3 fusion.7
  115.6 21.2 %all-reduce.2 = (f32[384]{0:T(512)S(1)}, f32[384]{0:T(512)S(1)}) all-reduce(f32[384]{0:T(512)S(1)} %get-tuple-element.73, f32[384]{0:T(512)S(1)} %get-tuple-element.74), channel_id=1, replica_groups=mesh['tile'=64,'head'=8] {'head'}, use_global_device_ids=true, to_apply=%region_1.2 | all-reduce | flops 768 | bytes 6144 | tf_op jit(solution)/shard_map/psum | solution.py:51
  136.8 1.2 fusion.12
  138.7 5.8 %collective-permute-start.2 = (bf16[64,640]{1,0:T(8,128)(2,1)}, bf16[64,640]{1,0:T(8,128)(2,1)S(1)}, u32[]{:S(2)}, u32[]{:S(2)}) collective-permute-start(bf16[64,640]{1,0:T(8,128)(2,1)} %get-tuple-element.67), channel_id=1, source_target_pairs={{0,8},{8,16},{16,24},{24,32},{32,40},{40,48},{48,56},{56,64},{64,7... | collective-permute-start | bytes 245768 | tf_op jit(solution)/shard_map/ppermute | solution.py:17
  144.6 1.9 collective-permute-start.3
  146.5 1.6 pad_dynamic-slice_fusion
  148.1 3.6 %collective-permute-start.4 = (bf16[64,640]{1,0:T(8,128)(2,1)}, bf16[64,640]{1,0:T(8,128)(2,1)S(1)}, u32[]{:S(2)}, u32[]{:S(2)}) collective-permute-start(bf16[64,640]{1,0:T(8,128)(2,1)} %get-tuple-element.65), channel_id=1, source_target_pairs={{0,8},{8,16},{16,24},{24,32},{32,40},{40,48},{48,56},{56,64},{64,7... | collective-permute-start | bytes 245768 | tf_op jit(solution)/shard_map/ppermute | solution.py:17
  151.8 1.9 collective-permute-start.5
  154.9 3.6 %collective-permute-start = (bf16[64]{0:T(256)(128)(2,1)}, bf16[64]{0:T(256)(128)(2,1)S(1)}, u32[]{:S(2)}, u32[]{:S(2)}) collective-permute-start(bf16[64]{0:T(256)(128)(2,1)} %compare_select_fusion.3), channel_id=1, source_target_pairs={{0,8},{8,16},{16,24},{24,32},{32,40},{40,48},{48,56},{56,64},{64,7... | collective-permute-start | bytes 392 | tf_op jit(solution)/shard_map/ppermute | solution.py:17
  159.2 2.0 fusion.9
  161.2 1.9 collective-permute-start.1
  163.1 3.0 %collective-permute-done.1 = bf16[64]{0:T(256)(128)(2,1)S(1)} collective-permute-done((bf16[64]{0:T(256)(128)(2,1)}, bf16[64]{0:T(256)(128)(2,1)S(1)}, u32[]{:S(2)}, u32[]{:S(2)}) %collective-permute-start.1) | collective-permute-done | bytes 160 | tf_op jit(solution)/shard_map/ppermute | solution.py:17
  166.2 1.5 gather_fusion.1
  167.7 10.7 %all-to-all-done.2 = bf16[64,2,8,640]{3,2,1,0:T(8,128)(2,1)S(1)} async-done(((bf16[64,2,8,640]{3,2,1,0:T(8,128)(2,1)}), bf16[64,2,8,640]{3,2,1,0:T(8,128)(2,1)S(1)}, u32[]{:S(2)}, u32[]{:S(2)}) %all-to-all-start.2) | async-done | bytes 1310752 | tf_op jit(solution)/shard_map/all_to_all | solution.py:87
  181.5 17.8 %while.10 = (s32[]{:T(128)}, bf16[5,384,128]{1,2,0:T(8,128)(2,1)S(1)}, pred[1024]{0:T(1024)(128)(4,1)S(1)}, s32[5]{0:T(128)S(1)}, bf16[384,640]{1,0:T(8,128)(2,1...) while((s32[]{:T(128)}, ...), condition=%wide.region_9.12_spmd, body=%wide.region_6.11_spmd.sunk | while | flops 204471552 | bytes 5548719 | solution.py:132
  182.7 1.4 fusion.22
  186.3 1.4 fusion.22
  189.9 1.4 fusion.22
  193.4 1.4 fusion.22
  197.0 1.4 fusion.22
  (75 shorter events, 18.5 us)
Async XLA Ops:
  0.0 34.0 %copy-start = (bf16[16,8,640]{2,1,0:T(8,128)(2,1)S(1)}, bf16[16,8,640]{2,1,0:T(8,128)(2,1)}, u32[]{:S(2)}) copy-start(bf16[16,8,640]{2,1,0:T(8,128)(2,1)} %param.22) | copy-start | bytes 491524
  34.0 0.9 copy-start.1
  106.3 8.0 %copy-start.4 = (bf16[384,640]{1,0:T(8,128)(2,1)S(1)}, bf16[384,640]{1,0:T(8,128)(2,1)}, u32[]{:S(2)}) copy-start(bf16[384,640]{1,0:T(8,128)(2,1)} %param.18) | copy-start | bytes 1474564
  106.3 30.5 %copy-start.6 = (f32[640]{0:T(1024)S(1)}, f32[640]{0:T(1024)}, u32[]{:S(2)}) copy-start(f32[640]{0:T(1024)} %param.21) | copy-start | bytes 7684
  106.3 72.2 %all-to-all-start.2 = ((bf16[64,2,8,640]{3,2,1,0:T(8,128)(2,1)}), bf16[64,2,8,640]{3,2,1,0:T(8,128)(2,1)S(1)}, u32[]{:S(2)}, u32[]{:S(2)}) async-start(bf16[64,2,8,640]{3,2,1,0:T(8,128)(2,1)} %get-tuple-element.69), calls=%async_computation.2 | async-start | bytes 2621440 | tf_op jit(solution)/shard_map/all_to_all | solution.py:87
  115.5 43.6 %copy-start.8 = (s32[64,1]{0,1:T(1,128)S(1)}, s32[64,1]{0,1:T(1,128)}, u32[]{:S(2)}) copy-start(s32[64,1]{0,1:T(1,128)} %param.26) | copy-start | bytes 772
  115.5 43.6 %copy-start.7 = (f32[640]{0:T(1024)S(1)}, f32[640]{0:T(1024)}, u32[]{:S(2)}) copy-start(f32[640]{0:T(1024)} %param.20) | copy-start | bytes 7684
  138.7 40.6 %collective-permute-start.2 = (bf16[64,640]{1,0:T(8,128)(2,1)}, bf16[64,640]{1,0:T(8,128)(2,1)S(1)}, u32[]{:S(2)}, u32[]{:S(2)}) collective-permute-start(bf16[64,640]{1,0:T(8,128)(2,1)} %get-tuple-element.67), channel_id=1, source_target_pairs={{0,8},{8,16},{16,24},{24,32},{32,40},{40,48},{48,56},{56,64},{64,7... | collective-permute-start | bytes 245768 | tf_op jit(solution)/shard_map/ppermute | solution.py:17
  144.6 34.8 %collective-permute-start.3 = (bf16[64,640]{1,0:T(8,128)(2,1)}, bf16[64,640]{1,0:T(8,128)(2,1)S(1)}, u32[]{:S(2)}, u32[]{:S(2)}) collective-permute-start(bf16[64,640]{1,0:T(8,128)(2,1)} %get-tuple-element.68), channel_id=1, source_target_pairs={{8,0},{16,8},{24,16},{32,24},{40,32},{48,40},{56,48},{64,56},{72,6... | collective-permute-start | bytes 245768 | tf_op jit(solution)/shard_map/ppermute | solution.py:17
  148.1 31.4 %collective-permute-start.4 = (bf16[64,640]{1,0:T(8,128)(2,1)}, bf16[64,640]{1,0:T(8,128)(2,1)S(1)}, u32[]{:S(2)}, u32[]{:S(2)}) collective-permute-start(bf16[64,640]{1,0:T(8,128)(2,1)} %get-tuple-element.65), channel_id=1, source_target_pairs={{0,8},{8,16},{16,24},{24,32},{32,40},{40,48},{48,56},{56,64},{64,7... | collective-permute-start | bytes 245768 | tf_op jit(solution)/shard_map/ppermute | solution.py:17
  151.8 27.7 %collective-permute-start.5 = (bf16[64,640]{1,0:T(8,128)(2,1)}, bf16[64,640]{1,0:T(8,128)(2,1)}, u32[]{:S(2)}, u32[]{:S(2)}) collective-permute-start(bf16[64,640]{1,0:T(8,128)(2,1)} %get-tuple-element.66), channel_id=1, source_target_pairs={{8,0},{16,8},{24,16},{32,24},{40,32},{48,40},{56,48},{64,56},{72,6... | collective-permute-start | bytes 245768 | tf_op jit(solution)/shard_map/ppermute | solution.py:17
  154.9 6.3 %collective-permute-start = (bf16[64]{0:T(256)(128)(2,1)}, bf16[64]{0:T(256)(128)(2,1)S(1)}, u32[]{:S(2)}, u32[]{:S(2)}) collective-permute-start(bf16[64]{0:T(256)(128)(2,1)} %compare_select_fusion.3), channel_id=1, source_target_pairs={{0,8},{8,16},{16,24},{24,32},{32,40},{40,48},{48,56},{56,64},{64,7... | collective-permute-start | bytes 392 | tf_op jit(solution)/shard_map/ppermute | solution.py:17
  161.2 4.9 %collective-permute-start.1 = (bf16[64]{0:T(256)(128)(2,1)}, bf16[64]{0:T(256)(128)(2,1)S(1)}, u32[]{:S(2)}, u32[]{:S(2)}) collective-permute-start(bf16[64]{0:T(256)(128)(2,1)} %compare_select_fusion.2), channel_id=1, source_target_pairs={{8,0},{16,8},{24,16},{32,24},{40,32},{48,40},{56,48},{64,56},{72,6... | collective-permute-start | bytes 392 | tf_op jit(solution)/shard_map/ppermute | solution.py:17
  167.7 11.4 %copy-start.2 = (bf16[64,8,640]{2,1,0:T(8,128)(2,1)S(1)}, bf16[64,8,640]{2,1,0:T(8,128)(2,1)}, u32[]{:S(2)}) copy-start(bf16[64,8,640]{2,1,0:T(8,128)(2,1)} %gather_fusion.1) | copy-start | bytes 1966084
  179.4 1.0 copy-start.3
  180.4 1.1 copy-start.5
where the time goes:
time: 203 us; the launch traced here: 200 us
  blocking collectives  121 us (60%)
  starting transfers between devices  26.2 us (13%)
  waiting for transfers between devices  13.8 us (7%)
  other arithmetic  13.1 us (6%)
  local copies, waits for them, and re-layouts  11.7 us (6%)
  matrix products  9.53 us (5%)
  loops' own time  3.38 us (2%)
    all_to_all x1, blocking collectives, per_device(): lax.all_to_all(picked_keys, 'tile', split_axis=0, concat_axis=0, tiled=True)  68.8 us
    all_to_all x1, blocking collectives, per_device(): lax.all_to_all(wanted, 'tile', split_axis=0, concat_axis=0, tiled=True)  31.2 us
    psum x1, blocking collectives, per_device(): lax.psum((row_squares(query_rows), row_squares(key_rows)), 'head')  21.2 us
    ppermute x6, starting transfers between devices, passed_along(): lax.ppermute(value, axis, [(source, source + steps) for source in range(f...  18.8 us
    all_to_all x1, waiting for transfers between devices, per_device(): lax.all_to_all(picked_values, 'tile', split_axis=0, concat_axis=0, tiled=...  10.7 us
    all_to_all x1, starting transfers between devices, per_device(): lax.all_to_all(picked_values, 'tile', split_axis=0, concat_axis=0, tiled=...  7.31 us
    dot_general x5, matrix products, one_head(): lax.dot_general(head_query, head_keys, (((1,), (1,)), ((), ())), preferre...  6.76 us
  transfers between devices with their start and end apart: 7, of which 2 were waited for; matrix products, arithmetic and copies ran while one was open for 5% of the time, Pallas kernels for 0%

commit v1 on v0

v1 whole, which is shorter than its diff:
```python
import functools
import math

import jax
import jax.numpy as jnp
from jax import lax
from jax.experimental import pallas as pl
from jax.experimental.pallas import tpu as pltpu
from jax.sharding import PartitionSpec as P

HEAD_DIM = 128
EDGE = 64
EPSILON = 1e-06
MESH = pl.DeviceIdType.MESH
NEG = -1e30
BF16 = jnp.bfloat16
F32 = jnp.float32
SCORE_SCALE = (1.0 / HEAD_DIM**0.5) * math.log2(math.e)


def kernel(
    tiles, nh, width,
    len_ref, ses_ref, own_ref, idx_ref, gq_ref, gk_ref,
    q_hbm, k_hbm, v_hbm, mk_hbm, mv_hbm, o_ref,
    kb, vb, cur_ka, cur_va, cur_kb, cur_vb,
    qr, kr, vr, qn, kn,
    ssrc, sbuf, wsrc, wrecv, mrecv, wsm,
    tail_k, tail_v, ek, ev,
    selk, selv, mkk, mvv,
    acc, mx, ls,
    rss, rrs, loc, sss, srs, wss, wrs, wls, mss, mrs, ess, ers, pss, prs,
):
    nz, half = tiles // 4, tiles // 8
    cap, wid = qr.shape
    heads = wid // HEAD_DIM
    t, h = lax.axis_index("tile"), lax.axis_index("head")
    z, sub = t // 4, lax.rem(t, 4)
    up, dn = lax.rem(t + 4, tiles), lax.rem(t + tiles - 4, tiles)
    right, left = lax.rem(t + 1, tiles), lax.rem(t + tiles - 1, tiles)

    def near(rel):
        other = sub + jnp.where(lax.rem(sub, 2) == 0, 1, -1) * (rel % 2)
        other = other + jnp.where(sub // 2 == 0, 2, -2) * (rel // 2)
        return z * 4 + other

    bar = pltpu.get_barrier_semaphore()
    greet = [up, dn, near(1), near(2), near(3), right, left]
    for n in greet:
        pl.semaphore_signal(bar, inc=1, device_id={"tile": n}, device_id_type=MESH)
    for i in range(1, nh):
        pl.semaphore_signal(bar, inc=1, device_id={"head": lax.rem(h + i, nh)}, device_id_type=MESH)
    pl.semaphore_wait(bar, len(greet) + nh - 1)

    def hop(d, s, x):
        buf, first = ((kb, mk_hbm), (vb, mv_hbm))[x]
        static = isinstance(s, int)
        if d == 0:
            src, dst, dev = s - 1, s, up
        else:
            src, dst, dev = nz + 1 - s, nz - s, dn
        return pltpu.make_async_remote_copy(
            src_ref=first if static and s == 1 else buf.at[src], dst_ref=buf.at[dst],
            send_sem=rss.at[d, s - 1, x], recv_sem=rrs.at[d, s - 1, x],
            device_id={"tile": dev}, device_id_type=MESH)

    for x in range(2):
        for d in range(2):
            hop(d, 1, x).start()

    loads = [
        pltpu.make_async_copy(a, b, loc.at[i])
        for i, (a, b) in enumerate(
            ((q_hbm, qr), (k_hbm, kr), (mk_hbm, kb.at[0]), (mv_hbm, vb.at[0]), (v_hbm, vr))
        )
    ]
    for copy in loads:
        copy.start()

    lane = lax.broadcasted_iota(jnp.int32, (1, 128), 1)

    def ask(r, carry):
        w0, w1 = carry
        hit, b = lane == own_ref[r], idx_ref[r]
        return (
            jnp.where(jnp.logical_and(hit, w0 < 0), b, w0),
            jnp.where(jnp.logical_and(hit, w0 >= 0), b, w1),
        )

    none = jnp.full((1, 128), -1, jnp.int32)
    w0, w1 = lax.fori_loop(0, own_ref.shape[0], ask, (none, none))
    length, session = len_ref[0], ses_ref[0]
    wsrc[0:1, :] = w0
    wsrc[1:2, :] = w1
    wsrc[2:3, :] = jnp.full((1, 128), length, jnp.int32)
    wsrc[3:4, :] = jnp.full((1, 128), session, jnp.int32)
    wsrc[4:8, :] = jnp.zeros((4, 128), jnp.int32)

    def tell(rel):
        return pltpu.make_async_remote_copy(
            src_ref=wsrc, dst_ref=wrecv.at[rel - 1], send_sem=wss.at[rel - 1], recv_sem=wrs.at[rel - 1],
            device_id={"tile": near(rel)}, device_id_type=MESH)

    def meta(side):
        return pltpu.make_async_remote_copy(
            src_ref=wsrc, dst_ref=mrecv.at[side], send_sem=mss.at[side], recv_sem=mrs.at[side],
            device_id={"tile": (right, left)[side]}, device_id_type=MESH)

    for rel in range(1, 4):
        tell(rel).start()
    meta(0).start()
    meta(1).start()

    loads[0].wait()
    loads[1].wait()

    def square_row(ref):
        part = jnp.zeros((cap, HEAD_DIM), F32)
        for c in range(heads):
            x = ref[:, c * HEAD_DIM : (c + 1) * HEAD_DIM].astype(F32)
            part = part + x * x
        return jnp.sum(part.T, axis=0, keepdims=True)

    ssrc[0:1, :] = square_row(qr)
    ssrc[1:2, :] = square_row(kr)
    sbuf[h] = ssrc[...]

    def share(i):
        return pltpu.make_async_remote_copy(
            src_ref=ssrc, dst_ref=sbuf.at[h], send_sem=sss.at[i - 1], recv_sem=srs.at[i - 1],
            device_id={"head": lax.rem(h + i, nh)}, device_id_type=MESH)

    def shared(i):
        return pltpu.make_async_remote_copy(
            src_ref=ssrc, dst_ref=sbuf.at[lax.rem(h + nh - i, nh)], send_sem=sss.at[i - 1], recv_sem=srs.at[i - 1],
            device_id={"head": lax.rem(h + i, nh)}, device_id_type=MESH)

    for i in range(1, nh):
        share(i).start()

    for i in range(heads):
        acc[i] = jnp.zeros((cap, HEAD_DIM), F32)
        mx[i] = jnp.full((cap, HEAD_DIM), NEG, F32)
        ls[i] = jnp.zeros((cap, HEAD_DIM), F32)

    @pl.when(t == 0)
    def _():
        ek[0:EDGE] = jnp.zeros((EDGE, wid), BF16)
        ev[0:EDGE] = jnp.zeros((EDGE, wid), BF16)

    @pl.when(t == tiles - 1)
    def _():
        ek[EDGE:] = jnp.zeros((EDGE, wid), BF16)
        ev[EDGE:] = jnp.zeros((EDGE, wid), BF16)

    to_smem = [pltpu.make_async_copy(wsrc, wsm.at[0], wls.at[0])]
    to_smem[0].start()
    for rel in range(1, 4):
        tell(rel).wait_recv()
        copy = pltpu.make_async_copy(wrecv.at[rel - 1], wsm.at[rel], wls.at[rel])
        copy.start()
        to_smem.append(copy)
    for copy in to_smem:
        copy.wait()

    def edge(side, x):
        src = ((tail_k, tail_v), (kn.at[pl.ds(0, EDGE)], vr.at[pl.ds(0, EDGE)]))[side][x]
        dst = (ek, ev)[x].at[pl.ds(side * EDGE, EDGE)]
        return pltpu.make_async_remote_copy(
            src_ref=src, dst_ref=dst, send_sem=ess.at[side, x], recv_sem=ers.at[side, x],
            device_id={"tile": (right, left)[side]}, device_id_type=MESH)

    def normalise():
        for i in range(1, nh):
            shared(i).wait_recv()
        total = sbuf[0]
        for i in range(1, nh):
            total = total + sbuf[i]
        factor = lax.rsqrt(total / width + EPSILON)
        for row, (raw, gain, out) in enumerate(((kr, gk_ref, kn), (qr, gq_ref, qn))):
            row = 1 - row
            wide = jnp.broadcast_to(factor[row : row + 1], (HEAD_DIM, cap)).T
            for c in range(heads):
                cols = slice(c * HEAD_DIM, (c + 1) * HEAD_DIM)
                out[:, cols] = (raw[:, cols].astype(F32) * wide * gain[:, cols]).astype(BF16)
        loads[4].wait()
        place = lax.broadcasted_iota(jnp.int32, (EDGE, cap), 0) + (length - EDGE)
        pick = (lax.broadcasted_iota(jnp.int32, (EDGE, cap), 1) == place).astype(F32).astype(BF16)
        tail_k[...] = jnp.dot(pick, kn[...], preferred_element_type=F32).astype(BF16)
        tail_v[...] = jnp.dot(pick, vr[...], preferred_element_type=F32).astype(BF16)

        @pl.when(t < tiles - 1)
        def _():
            for x in range(2):
                edge(0, x).start()

        @pl.when(t > 0)
        def _():
            for x in range(2):
                edge(1, x).start()

    def update(i, keys, values, bias):
        cols = pl.ds(pl.multiple_of(i * HEAD_DIM, HEAD_DIM), HEAD_DIM)
        scores = lax.dot_general(qn[:, cols], keys(cols), (((1,), (1,)), ((), ())), preferred_element_type=F32)
        scores = scores * SCORE_SCALE + bias
        before = mx[i]
        now = jnp.maximum(before, jnp.max(scores, axis=1, keepdims=True))
        expo = jnp.exp2(scores - now[:, :1])
        keep = jnp.exp2(before - now)
        mx[i] = now
        ls[i] = ls[i] * keep + jnp.sum(expo, axis=1, keepdims=True)
        acc[i] = acc[i] * keep + jnp.dot(expo.astype(BF16), values(cols), preferred_element_type=F32)

    def own_attention(i):
        spot = lax.broadcasted_iota(jnp.int32, (1, cap), 1)
        ok_own = jnp.where(spot < length, 0.0, NEG).astype(F32)
        slot = lax.broadcasted_iota(jnp.int32, (1, 2 * EDGE), 1)
        ll, lsess = mrecv[0, 2:3, :], mrecv[0, 3:4, :]
        rl, rsess = mrecv[1, 2:3, :], mrecv[1, 3:4, :]
        from_left = (slot < EDGE) & (lsess == jnp.where(t > 0, session, -1)) & (slot >= EDGE - ll)
        from_right = (slot >= EDGE) & (rsess == jnp.where(t < tiles - 1, session, -1)) & (slot - EDGE < rl)
        ok_edge = jnp.where(from_left | from_right, 0.0, NEG).astype(F32)
        update(
            i,
            lambda c: jnp.concatenate([kn[:, c], ek[:, c]], 0),
            lambda c: jnp.concatenate([vr[:, c], ev[:, c]], 0),
            jnp.concatenate([ok_own, ok_edge], 1),
        )

    def origin(r):
        return lax.rem(z + nz - r, nz)

    def pick_out(r, src_k, src_v):
        owner = origin(r) * 4 + sub
        for rel in range(4):
            for slot in range(2):
                want = jnp.maximum(wsm[rel, slot, owner], 0)
                if rel == 0:
                    mkk[r, slot] = src_k[want]
                    mvv[r, slot] = src_v[want]
                else:
                    selk[rel - 1, r, slot] = src_k[want]
                    selv[rel - 1, r, slot] = src_v[want]

    def give(rel, r, x):
        src, dst = ((selk, mkk), (selv, mvv))[x]
        return pltpu.make_async_remote_copy(
            src_ref=src.at[rel - 1, r], dst_ref=dst.at[r, pl.ds(2 * rel, 2)],
            send_sem=pss.at[rel - 1, r, x], recv_sem=prs.at[rel - 1, r, x],
            device_id={"tile": near(rel)}, device_id_type=MESH)

    def hand_out(r, src_k, src_v):
        pick_out(r, src_k, src_v)
        for rel in (2, 3, 1):
            for x in range(2):
                give(rel, r, x).start()

    def chunk(ra, rb):
        for r in (ra, rb):
            for rel in range(1, 4):
                for x in range(2):
                    give(rel, r, x).wait_recv()
        group = lane // 8
        bias = jnp.zeros((1, 128), F32)
        for j, r in enumerate((ra, rb)):
            for rel in range(4):
                for slot in range(2):
                    want = wsm[0, slot, origin(r) * 4 + near(rel) - z * 4]
                    miss = jnp.where(want < 0, NEG, 0.0).astype(F32)
                    bias = jnp.where(group == j * 8 + rel * 2 + slot, miss, bias)

        def rows(ref, c):
            return jnp.concatenate([ref[r, :, :, c].reshape(64, HEAD_DIM) for r in (ra, rb)], 0)

        @pl.loop(0, heads)
        def _(i):
            update(i, lambda c: rows(mkk, c), lambda c: rows(mvv, c), bias)

    loads[2].wait()
    loads[3].wait()
    cur_ka[...] = kb[0]
    cur_va[...] = vb[0]
    hand_out(0, cur_ka, cur_va)

    def arrived(s, x, last):
        for d in range(2):
            hop(d, s, x).wait_recv()
            if not last or d == x:
                hop(d, s + 1, x).start()

    def take(s):
        cur_ka[...] = kb[s]
        cur_va[...] = vb[s]
        cur_kb[...] = kb[nz - s]
        cur_vb[...] = vb[nz - s]
        hand_out(s, cur_ka, cur_va)
        hand_out(nz - s, cur_kb, cur_vb)

    arrived(1, 0, half == 2)
    normalise()
    arrived(1, 1, half == 2)
    take(1)
    meta(0).wait_recv()
    meta(1).wait_recv()
    for side, there in ((0, t > 0), (1, t < tiles - 1)):

        @pl.when(there)
        def _(side=side):
            for x in range(2):
                edge(side, x).wait_recv()

    @pl.loop(2, half - 1)
    def _(s):
        arrived(s, 0, False)
        pl.when(s - 2 < heads)(lambda: own_attention(s - 2))
        arrived(s, 1, False)
        take(s)
        chunk(s - 1, nz - s + 1)

    if half > 2:
        arrived(half - 1, 0, True)
        arrived(half - 1, 1, True)
        take(half - 1)
        chunk(half - 2, nz - half + 2)
    for i in range(max(0, half - 3), heads):
        own_attention(i)
    hop(0, half, 0).wait_recv()
    cur_ka[...] = kb[half]
    hop(1, half, 1).wait_recv()
    cur_va[...] = vb[half]
    hand_out(half, cur_ka, cur_va)
    chunk(half - 1, nz - half + 1)
    chunk(0, half)

    live = lax.broadcasted_iota(jnp.int32, (cap, HEAD_DIM), 0) < length
    for i in range(heads):
        out = jnp.where(live, acc[i] / ls[i], 0.0)
        o_ref[:, i * HEAD_DIM : (i + 1) * HEAD_DIM] = out.astype(BF16)

    for s in range(1, half + 1):
        for x in range(2):
            for d in range(2):
                if s < half or d == x:
                    hop(d, s, x).wait_send()
    for rel in range(1, 4):
        tell(rel).wait_send()
        for r in range(nz):
            for x in range(2):
                give(rel, r, x).wait_send()
    for i in range(1, nh):
        share(i).wait_send()
    for side, there in ((0, t < tiles - 1), (1, t > 0)):
        meta(side).wait_send()

        @pl.when(there)
        def _(side=side):
            for x in range(2):
                edge(side, x).wait_send()


def per_device(tiles, nh, width, q, k, v, gq, gk, mk, mv, tile_len, session, owner, index):
    nz, half = tiles // 4, tiles // 8
    (cap, wid), (blocks, rows, _) = q.shape, mk.shape
    heads = wid // HEAD_DIM
    smem = pl.BlockSpec(memory_space=pltpu.SMEM)
    vmem = pl.BlockSpec(memory_space=pltpu.VMEM)
    any_space = pl.BlockSpec(memory_space=pl.ANY)
    sem = pltpu.SemaphoreType.DMA
    tile = pltpu.VMEM((cap, wid), BF16)
    state = pltpu.VMEM((heads, cap, HEAD_DIM), F32)
    block = pltpu.VMEM((blocks, rows, wid), BF16)
    edge = pltpu.VMEM((EDGE, wid), BF16)
    return pl.pallas_call(
        functools.partial(kernel, tiles, nh, width),
        out_shape=jax.ShapeDtypeStruct((cap, wid), BF16),
        in_specs=[smem] * 4 + [vmem] * 2 + [any_space] * 5,
        out_specs=vmem,
        scratch_shapes=[
            pltpu.VMEM((nz, blocks, rows, wid), BF16),
            pltpu.VMEM((nz, blocks, rows, wid), BF16),
            block, block, block, block,
            tile, tile, tile, tile, tile,
            pltpu.VMEM((2, cap), F32),
            pltpu.VMEM((nh, 2, cap), F32),
            pltpu.VMEM((8, 128), jnp.int32),
            pltpu.VMEM((3, 8, 128), jnp.int32),
            pltpu.VMEM((2, 8, 128), jnp.int32),
            pltpu.SMEM((4, 8, 128), jnp.int32),
            edge, edge,
            pltpu.VMEM((2 * EDGE, wid), BF16),
            pltpu.VMEM((2 * EDGE, wid), BF16),
            pltpu.VMEM((3, nz, 2, rows, wid), BF16),
            pltpu.VMEM((3, nz, 2, rows, wid), BF16),
            pltpu.VMEM((nz, 8, rows, wid), BF16),
            pltpu.VMEM((nz, 8, rows, wid), BF16),
            state, state, state,
            sem((2, half, 2)), sem((2, half, 2)), sem((5,)),
            sem((max(1, nh - 1),)), sem((max(1, nh - 1),)),
            sem((3,)), sem((3,)), sem((4,)),
            sem((2,)), sem((2,)), sem((2, 2)), sem((2, 2)),
            sem((3, nz, 2)), sem((3, nz, 2)),
        ],
        compiler_params=pltpu.CompilerParams(
            collective_id=0, has_side_effects=True, vmem_limit_bytes=60 * 1024 * 1024
        ),
        name="tile_attention",
    )(
        tile_len, session, owner.reshape(-1), index, gq.reshape(1, -1), gk.reshape(1, -1),
        q, k, v, mk, mv,
    )


def solution(mesh):
    in_specs = (
        P("tile", "head"),
        P("tile", "head"),
        P("tile", "head"),
        P("head"),
        P("head"),
        P("tile", None, "head"),
        P("tile", None, "head"),
        P("tile"),
        P("tile"),
        P("tile", None),
        P("tile"),
    )
    tiles, nh = mesh.shape["tile"], mesh.shape["head"]

    def whole(q, *rest):
        body = functools.partial(per_device, tiles, nh, q.shape[1])
        return jax.shard_map(
            body, mesh=mesh, in_specs=in_specs, out_specs=P("tile", "head"), check_vma=False
        )(q, *rest)

    return whole
```

time: 203 us -> 86.6 us (0.43)
  blocking collectives: 121 us -> 0 us
  Pallas kernels: 0 us -> 81.4 us
  starting transfers between devices: 26.2 us -> 0 us
  waiting for transfers between devices: 13.8 us -> 0 us
  other arithmetic: 13.1 us -> 0 us
  matrix products: 9.53 us -> 0 us
  local copies, waits for them, and re-layouts: 11.7 us -> 3.12 us
  loops' own time: 3.38 us -> 0 us
    all_to_all x2 -> x0, blocking collectives: 100 us -> none  [the longest x1 68.8 us: per_device(): lax.all_to_all(picked_keys, 'tile', split_axis=0, concat_axis=0, tiled=True)]
    pallas_call x0 -> x1, Pallas kernels: none -> 81.4 us  [per_device(): pl.pallas_call(functools.partial(kernel, tiles, nh, width), out_shape=jax...]
    psum x1 -> x0, blocking collectives: 21.2 us -> none  [per_device(): lax.psum((row_squares(query_rows), row_squares(key_rows)), 'head')]
    ppermute x6 -> x0, starting transfers between devices: 18.8 us -> none  [passed_along(): lax.ppermute(value, axis, [(source, source + steps) for source in range(f...]
    all_to_all x1 -> x0, waiting for transfers between devices: 10.7 us -> none  [per_device(): lax.all_to_all(picked_values, 'tile', split_axis=0, concat_axis=0, tiled=...]
    dot_general x10 -> x0, matrix products: 9.53 us -> none  [the longest x5 6.76 us: one_head(): lax.dot_general(head_query, head_keys, (((1,), (1,)), ((), ())), preferre...]
    all_to_all x1 -> x0, starting transfers between devices: 7.31 us -> none  [per_device(): lax.all_to_all(picked_values, 'tile', split_axis=0, concat_axis=0, tiled=...]
    dynamic_slice x7 -> x0, local copies, waits for them, and re-layouts: 5.28 us -> none  [the longest x5 2.93 us: per_device(): outputs = lax.map(one_head, jnp.arange(heads_here, dtype=jnp.int32))]
  transfers between devices with their start and end apart: 7 -> 0, of which waited for: 2 -> 0; matrix products, arithmetic and copies ran while one was open for 5% -> 0% of each run, Pallas kernels for 0% -> 0%
where the time goes in v1:
time: 86.6 us; the launch traced here: 85.8 us
  Pallas kernels  81.4 us (94%)
  local copies, waits for them, and re-layouts  3.12 us (4%)
  between operations  1.34 us (2%)
    pallas_call x1, Pallas kernels, per_device(): pl.pallas_call(functools.partial(kernel, tiles, nh, width), out_shape=jax...  81.4 us
    unnamed x5, local copies, waits for them, and re-layouts  1.94 us

profile of v1, /device:TPU:1, one launch (start us, length us, event | category | flops | bytes accessed | tf_op | source)
XLA Modules:
  0.0 85.8 jit_solution(966291831382954332)
XLA Ops:
  0.0 0.0 copy-start
  1.3 0.0 copy-start.1
  1.3 0.0 copy-done
  1.3 0.6 reshape.10.gq_ref
  1.9 0.1 copy-done.1
  2.0 0.6 reshape.11.gk_ref
  2.6 81.4 %tile_attention.1 = bf16[384,640]{1,0:T(8,128)(2,1)} custom-call(s32[1]{0:T(128)S(6)} %copy.13.len_ref, s32[1]{0:T(128)S(6)} %copy.14.ses_ref, s32[64]{0:T(128)} %bitcast.1, s32[64]{0:T(128)} %idx_ref.1, f32[1,640]{1,0:T(1,128)} %reshape.10.gq_ref, f32[1,640]{1,0:T(1,128)} %reshape.11.gk_ref, bf16[384,640]{1,0:T(8,128)(2,1)} %q_hbm.1, ...), custom_call_target="tpu_custom_call" | custom-call | tf_op jit(solution)/shard_map/tile_attention/pallas_call | solution.py:372
  84.0 1.9 %copy.15 = bf16[384,640]{1,0:T(8,128)(2,1)} copy(bf16[384,640]{1,0:T(8,128)(2,1)} %tile_attention.1) | data formatting | bytes 983040
Async XLA Ops:
  0.0 1.3 %copy-start = (f32[640]{0:T(1024)S(1)}, f32[640]{0:T(1024)}, u32[]{:S(2)}) copy-start(f32[640]{0:T(1024)} %param.14) | copy-start | bytes 7684
  1.3 0.7 copy-start.1

commit v2 on v1

v2 whole, which is shorter than its diff:
```python
import functools
import math

import jax
import jax.numpy as jnp
from jax import lax
from jax.experimental import pallas as pl
from jax.experimental.pallas import tpu as pltpu
from jax.sharding import PartitionSpec as P

HEAD_DIM = 128
EDGE = 64
EPSILON = 1e-06
MESH = pl.DeviceIdType.MESH
NEG = -1e30
BF16 = jnp.bfloat16
F32 = jnp.float32
SCORE_SCALE = (1.0 / HEAD_DIM**0.5) * math.log2(math.e)


def kernel(
    tiles, nh, width,
    msrc, own_ref, idx_ref, gq_hbm, gk_hbm,
    q_hbm, k_hbm, v_hbm, mk_hbm, mv_hbm, o_ref,
    kvb, cur_ka, cur_va, cur_kb, cur_vb,
    qr, kr, vr, qn, kn,
    gq_ref, gk_ref,
    ssrc, sbuf, shalf, sother, wsrc, wnear, wfar, mrecv, snear, sfar,
    tail, ekv, sel, far, mkk, mvv,
    acc, mx, ls,
    out_sem, hop_sem, loc, table_sem, near_sem, edge_out, edge_in, tab_loc,
):
    nz, half = tiles // 4, tiles // 8
    full = half - 2
    cap, wid = qr.shape
    heads = wid // HEAD_DIM
    t, h = lax.axis_index("tile"), lax.axis_index("head")
    z, sub = t // 4, lax.rem(t, 4)
    up, dn = lax.rem(t + 4, tiles), lax.rem(t + tiles - 4, tiles)
    right, left = lax.rem(t + 1, tiles), lax.rem(t + tiles - 1, tiles)

    def near(rel):
        other = sub + jnp.where(lax.rem(sub, 2) == 0, 1, -1) * (rel % 2)
        other = other + jnp.where(sub // 2 == 0, 2, -2) * (rel // 2)
        return z * 4 + other

    def landed(ref, semaphore):
        pltpu.make_async_copy(ref, ref, semaphore).wait()

    bar = pltpu.get_barrier_semaphore()
    steps = (1, -1, 2, -2)

    def at(dz, rel):
        return lax.rem(z + dz + nz, nz) * 4 + near(rel) - z * 4

    greet = [{"tile": near(rel)} for rel in range(1, 4)]
    greet += [{"tile": at(dz, rel)} for dz in steps for rel in range(4)]
    greet += [{"head": lax.rem(h + 2 * i, nh)} for i in range(1, nh // 2)]
    hpair = h + jnp.where(lax.rem(h, 2) == 0, 1, -1)
    greet += [{"head": hpair}]
    for n in greet:
        pl.semaphore_signal(bar, inc=1, device_id=n, device_id_type=MESH)
    pl.semaphore_wait(bar, len(greet))

    def hop(d, s, x):
        first = (mk_hbm, mv_hbm)[x]
        static = isinstance(s, int)
        if d == 0:
            src, dst, dev = s - 1, s, up
        else:
            src, dst, dev = nz + 1 - s, nz - s, dn
        return pltpu.make_async_remote_copy(
            src_ref=first if static and s == 1 else kvb.at[x * nz + src], dst_ref=kvb.at[x * nz + dst],
            send_sem=out_sem.at[0], recv_sem=hop_sem.at[d, s - 1, x],
            device_id={"tile": dev}, device_id_type=MESH)

    for x in range(2):
        for d in range(2):
            hop(d, 1, x).start()

    loads = [
        pltpu.make_async_copy(a, b, loc.at[i])
        for i, (a, b) in enumerate((
            (q_hbm, qr), (k_hbm, kr), (mk_hbm, kvb.at[0]), (mv_hbm, kvb.at[nz]), (v_hbm, vr),
            (gq_hbm, gq_ref), (gk_hbm, gk_ref),
        ))
    ]
    for copy in loads:
        copy.start()

    lane = lax.broadcasted_iota(jnp.int32, (1, 128), 1)

    def ask(r, carry):
        w0, w1 = carry
        hit, b = lane == own_ref[r], idx_ref[r]
        return (
            jnp.where(jnp.logical_and(hit, w0 < 0), b, w0),
            jnp.where(jnp.logical_and(hit, w0 >= 0), b, w1),
        )

    none = jnp.full((1, 128), -1, jnp.int32)
    w0, w1 = lax.fori_loop(0, own_ref.shape[0], ask, (none, none))
    length, session = msrc[0:1, 0:1], msrc[1:2, 0:1]
    wsrc[0:1, :] = w0
    wsrc[1:2, :] = w1

    def tell(rel):
        return pltpu.make_async_remote_copy(
            src_ref=wsrc, dst_ref=wnear.at[rel], send_sem=out_sem.at[1], recv_sem=table_sem.at[0],
            device_id={"tile": near(rel)}, device_id_type=MESH)

    def tell_far(i, rel):
        return pltpu.make_async_remote_copy(
            src_ref=wsrc, dst_ref=wfar.at[(i ^ 1) * 4 + rel], send_sem=out_sem.at[2], recv_sem=table_sem.at[1],
            device_id={"tile": at(steps[i], rel)}, device_id_type=MESH)

    def meta(side):
        return pltpu.make_async_remote_copy(
            src_ref=msrc, dst_ref=mrecv.at[side], send_sem=out_sem.at[3], recv_sem=table_sem.at[2],
            device_id={"tile": (right, left)[side]}, device_id_type=MESH)

    wnear[0] = wsrc[...]
    for rel in range(1, 4):
        tell(rel).start()
    meta(0).start()
    meta(1).start()
    for i in range(4):
        for rel in range(4):
            tell_far(i, rel).start()

    loads[0].wait()
    loads[1].wait()

    def square_row(ref):
        part = jnp.zeros((cap, HEAD_DIM), F32)
        for c in range(heads):
            x = ref[:, c * HEAD_DIM : (c + 1) * HEAD_DIM].astype(F32)
            part = part + x * x
        return jnp.sum(part.T, axis=0, keepdims=True)

    ssrc[0:1, :] = square_row(qr)
    ssrc[1:2, :] = square_row(kr)
    sbuf[h // 2] = ssrc[...]

    def share(i):
        return pltpu.make_async_remote_copy(
            src_ref=ssrc, dst_ref=sbuf.at[h // 2], send_sem=out_sem.at[4], recv_sem=table_sem.at[3],
            device_id={"head": lax.rem(h + 2 * i, nh)}, device_id_type=MESH)

    for i in range(1, nh // 2):
        share(i).start()

    pair = pltpu.make_async_remote_copy(
        src_ref=shalf, dst_ref=sother, send_sem=out_sem.at[5], recv_sem=table_sem.at[4],
        device_id={"head": hpair}, device_id_type=MESH)

    for i in range(heads):
        acc[i] = jnp.zeros((cap, HEAD_DIM), F32)
        mx[i] = jnp.full((cap, HEAD_DIM), NEG, F32)
        ls[i] = jnp.zeros((cap, HEAD_DIM), F32)

    @pl.when(t == 0)
    def _():
        ekv[0] = jnp.zeros((2, EDGE, wid), BF16)

    @pl.when(t == tiles - 1)
    def _():
        ekv[1] = jnp.zeros((2, EDGE, wid), BF16)

    landed(wnear.at[pl.ds(1, 3)], table_sem.at[0])
    copy = pltpu.make_async_copy(wnear, snear, tab_loc.at[0])
    copy.start()
    copy.wait()

    def edge(side, x):
        src = (tail.at[x], (kn, vr)[x].at[pl.ds(0, EDGE)])[side]
        return pltpu.make_async_remote_copy(
            src_ref=src, dst_ref=ekv.at[side, x], send_sem=edge_out.at[side], recv_sem=edge_in.at[side],
            device_id={"tile": (right, left)[side]}, device_id_type=MESH)

    def normalise():
        pair.wait_recv()
        loads[5].wait()
        loads[6].wait()
        factor = lax.rsqrt((shalf[...] + sother[...]) / width + EPSILON)
        for row, (raw, gain, out) in enumerate(((kr, gk_ref, kn), (qr, gq_ref, qn))):
            row = 1 - row
            wide = jnp.broadcast_to(factor[row : row + 1], (HEAD_DIM, cap)).T
            for c in range(heads):
                cols = slice(c * HEAD_DIM, (c + 1) * HEAD_DIM)
                out[:, cols] = (raw[:, cols].astype(F32) * wide * gain[cols].reshape(1, HEAD_DIM)).astype(BF16)
        loads[4].wait()
        place = lax.broadcasted_iota(jnp.int32, (EDGE, cap), 0) + (length - EDGE)
        pick = (lax.broadcasted_iota(jnp.int32, (EDGE, cap), 1) == place).astype(F32).astype(BF16)
        tail[0] = jnp.dot(pick, kn[...], preferred_element_type=F32).astype(BF16)
        tail[1] = jnp.dot(pick, vr[...], preferred_element_type=F32).astype(BF16)

        @pl.when(t < tiles - 1)
        def _():
            for x in range(2):
                edge(0, x).start()

        @pl.when(t > 0)
        def _():
            for x in range(2):
                edge(1, x).start()

    def update(i, keys, values, bias):
        cols = pl.ds(pl.multiple_of(i * HEAD_DIM, HEAD_DIM), HEAD_DIM)
        scores = lax.dot_general(qn[:, cols], keys(cols), (((1,), (1,)), ((), ())), preferred_element_type=F32)
        scores = scores * SCORE_SCALE + bias
        before = mx[i]
        now = jnp.maximum(before, jnp.max(scores, axis=1, keepdims=True))
        expo = jnp.exp2(scores - now[:, :1])
        keep = jnp.exp2(before - now)
        mx[i] = now
        ls[i] = ls[i] * keep + jnp.sum(expo, axis=1, keepdims=True)
        acc[i] = acc[i] * keep + jnp.dot(expo.astype(BF16), values(cols), preferred_element_type=F32)

    def own_attention(i):
        spot = lax.broadcasted_iota(jnp.int32, (1, cap), 1)
        ok_own = jnp.where(spot < length, 0.0, NEG).astype(F32)
        slot = lax.broadcasted_iota(jnp.int32, (1, 2 * EDGE), 1)
        ll, lsess = mrecv[0, 0:1, :], mrecv[0, 1:2, :]
        rl, rsess = mrecv[1, 0:1, :], mrecv[1, 1:2, :]
        from_left = (slot < EDGE) & (lsess == jnp.where(t > 0, session, -1)) & (slot >= EDGE - ll)
        from_right = (slot >= EDGE) & (rsess == jnp.where(t < tiles - 1, session, -1)) & (slot - EDGE < rl)
        ok_edge = jnp.where(from_left | from_right, 0.0, NEG).astype(F32)
        update(
            i,
            lambda c: jnp.concatenate([kn[:, c], ekv[0, 0, :, c], ekv[1, 0, :, c]], 0),
            lambda c: jnp.concatenate([vr[:, c], ekv[0, 1, :, c], ekv[1, 1, :, c]], 0),
            jnp.concatenate([ok_own, ok_edge], 1),
        )

    def origin(r):
        return lax.rem(z + nz - r, nz)

    def hand_out(r, x, src):
        owner = origin(r) * 4 + sub
        for rel in (2, 3, 1, 0):
            out = (mkk, mvv)[x].at[r, pl.ds(0, 2)] if rel == 0 else sel.at[(x * 3 + rel - 1) * nz + r]
            for slot in range(2):
                out[slot] = src[jnp.maximum(snear[rel, slot, owner], 0)]
            if rel > 0:
                pltpu.make_async_remote_copy(
                    src_ref=sel.at[(x * 3 + rel - 1) * nz + r], dst_ref=(mkk, mvv)[x].at[r, pl.ds(2 * rel, 2)],
                    send_sem=out_sem.at[6], recv_sem=near_sem.at[r],
                    device_id={"tile": near(rel)}, device_id_type=MESH).start()

    def far_out(d, x, src):
        owner = origin(full if d == 0 else nz - full) * 4 + sub
        for far_by in (1, 2) if d == x else (1,):
            i, r = (far_by - 1) * 2 + d, (full + far_by) if d == 0 else nz - full - far_by
            for rel in range(4):
                place = (d * 2 + x if far_by == 1 else 4 + d) * 4 + rel
                for slot in range(2):
                    far[place, slot] = src[jnp.maximum(sfar[i * 4 + rel, slot, owner], 0)]
                pltpu.make_async_remote_copy(
                    src_ref=far.at[place], dst_ref=(mkk, mvv)[x].at[r, pl.ds(2 * rel, 2)],
                    send_sem=out_sem.at[7], recv_sem=near_sem.at[r],
                    device_id={"tile": at(steps[i], rel)}, device_id_type=MESH).start()

    def chunk(slots, beyond, loop):
        for r in slots:
            away = beyond and isinstance(r, int) and full < r < nz - full
            landed(sel.at[pl.ds(0, 8 if away else 6)], near_sem.at[r])
        group = lane // 8
        biases = []
        for pair_of in (slots[i : i + 2] for i in range(0, len(slots), 2)):
            bias = jnp.full((1, 128), NEG, F32)
            for j, r in enumerate(pair_of):
                for rel in range(4):
                    for slot in range(2):
                        want = snear[0, slot, origin(r) * 4 + near(rel) - z * 4]
                        miss = jnp.where(want < 0, NEG, 0.0).astype(F32)
                        bias = jnp.where(group == j * 8 + rel * 2 + slot, miss, bias)
            biases.append(bias[:, : 64 * len(pair_of)])
        bias = biases[0] if len(biases) == 1 else jnp.concatenate(biases, 1)

        def rows(ref, c):
            return jnp.concatenate([ref[r, :, :, c].reshape(64, HEAD_DIM) for r in slots], 0)

        def one(i):
            update(i, lambda c: rows(mkk, c), lambda c: rows(mvv, c), bias)

        if loop:
            pl.loop(0, heads)(one)
        else:
            for i in range(heads):
                one(i)

    loads[2].wait()
    loads[3].wait()
    cur_ka[...] = kvb[0]
    cur_va[...] = kvb[nz]
    hand_out(0, 0, cur_ka)
    hand_out(0, 1, cur_va)

    def arrived(s, x):
        for d in range(2):
            hop(d, s, x).wait_recv()
            hop(d, s + 1, x).start()

    def take(s, x):
        up_cur, dn_cur = ((cur_ka, cur_kb), (cur_va, cur_vb))[x]
        up_cur[...] = kvb[x * nz + s]
        dn_cur[...] = kvb[x * nz + nz - s]
        hand_out(s, x, up_cur)
        hand_out(nz - s, x, dn_cur)

    def halves():
        landed(sbuf.at[pl.ds(0, nh // 2 - 1)], table_sem.at[3])
        total = sbuf[0]
        for i in range(1, nh // 2):
            total = total + sbuf[i]
        shalf[...] = total
        pair.start()

    arrived(1, 0)
    take(1, 0)
    halves()
    arrived(1, 1)
    take(1, 1)
    normalise()
    arrived(2, 0)
    take(2, 0)
    arrived(2, 1)
    take(2, 1)
    chunk((1, nz - 1), False, True)
    landed(mrecv, table_sem.at[2])
    for side, there in ((0, t > 0), (1, t < tiles - 1)):

        @pl.when(there)
        def _(side=side):
            landed(ekv.at[side], edge_in.at[side])

    @pl.loop(3, full)
    def _(s):
        arrived(s, 0)
        take(s, 0)
        pl.when(s - 3 < heads)(lambda: own_attention(s - 3))
        arrived(s, 1)
        take(s, 1)
        chunk((s - 1, nz - s + 1), False, True)

    landed(wfar, table_sem.at[1])
    copy = pltpu.make_async_copy(wfar, sfar, tab_loc.at[1])
    copy.start()
    copy.wait()
    for x, (up_cur, dn_cur) in enumerate(((cur_ka, cur_kb), (cur_va, cur_vb))):
        hop(0, full, x).wait_recv()
        hop(1, full, x).wait_recv()
        take(full, x)
        far_out(0, x, up_cur)
        far_out(1, x, dn_cur)
    chunk((full - 1, nz - full + 1), False, True)
    for i in range(max(0, full - 3), heads):
        own_attention(i)
    chunk((0,), False, True)
    chunk((full, nz - full, half - 1, nz - half + 1, half), True, False)
    for i in range(heads):
        o_ref[:, i * HEAD_DIM : (i + 1) * HEAD_DIM] = (acc[i] / ls[i]).astype(BF16)

    landed(kvb.at[pl.ds(0, 4 * full)], out_sem.at[0])
    landed(wnear.at[pl.ds(0, 3)], out_sem.at[1])
    landed(wfar, out_sem.at[2])
    landed(mrecv, out_sem.at[3])
    landed(sbuf.at[pl.ds(0, nh // 2 - 1)], out_sem.at[4])
    pair.wait_send()
    landed(sel.at[pl.ds(0, 6 * (2 * full + 1))], out_sem.at[6])
    landed(far, out_sem.at[7])
    for side, there in ((0, t < tiles - 1), (1, t > 0)):

        @pl.when(there)
        def _(side=side):
            landed(ekv.at[side], edge_out.at[side])


def per_device(tiles, nh, width, q, k, v, gq, gk, mk, mv, tile_len, session, owner, index):
    nz, half = tiles // 4, tiles // 8
    (cap, wid), (blocks, rows, _) = q.shape, mk.shape
    heads = wid // HEAD_DIM
    smem = pl.BlockSpec(memory_space=pltpu.SMEM)
    vmem = pl.BlockSpec(memory_space=pltpu.VMEM)
    hbm = pl.BlockSpec(memory_space=pltpu.HBM)
    sem = pltpu.SemaphoreType.DMA
    tile = pltpu.VMEM((cap, wid), BF16)
    state = pltpu.VMEM((heads, cap, HEAD_DIM), F32)
    block = pltpu.VMEM((blocks, rows, wid), BF16)
    meta = jnp.where(lax.broadcasted_iota(jnp.int32, (2, 128), 0) == 0, tile_len[0], session[0])
    attended = pl.pallas_call(
        functools.partial(kernel, tiles, nh, width),
        out_shape=jax.ShapeDtypeStruct((cap, wid), BF16),
        in_specs=[vmem] + [smem] * 2 + [hbm] * 7,
        out_specs=vmem,
        scratch_shapes=[
            pltpu.VMEM((2 * nz, blocks, rows, wid), BF16),
            block, block, block, block,
            tile, tile, tile, tile, tile,
            pltpu.VMEM((wid,), F32),
            pltpu.VMEM((wid,), F32),
            pltpu.VMEM((2, cap), F32),
            pltpu.VMEM((nh // 2, 2, cap), F32),
            pltpu.VMEM((2, cap), F32),
            pltpu.VMEM((2, cap), F32),
            pltpu.VMEM((2, 128), jnp.int32),
            pltpu.VMEM((4, 2, 128), jnp.int32),
            pltpu.VMEM((16, 2, 128), jnp.int32),
            pltpu.VMEM((2, 2, 128), jnp.int32),
            pltpu.SMEM((4, 2, 128), jnp.int32),
            pltpu.SMEM((16, 2, 128), jnp.int32),
            pltpu.VMEM((2, EDGE, wid), BF16),
            pltpu.VMEM((2, 2, EDGE, wid), BF16),
            pltpu.VMEM((6 * nz, 2, rows, wid), BF16),
            pltpu.VMEM((24, 2, rows, wid), BF16),
            pltpu.VMEM((nz, 8, rows, wid), BF16),
            pltpu.VMEM((nz, 8, rows, wid), BF16),
            state, state, state,
            sem((8,)), sem((2, half - 2, 2)), sem((7,)), sem((5,)), sem((nz,)), sem((2,)), sem((2,)), sem((2,)),
        ],
        compiler_params=pltpu.CompilerParams(
            collective_id=0, has_side_effects=True, vmem_limit_bytes=60 * 1024 * 1024
        ),
        name="tile_attention",
    )(
        meta, owner.reshape(-1), index, gq, gk, q, k, v, mk, mv,
    )
    live = lax.broadcasted_iota(jnp.int32, (cap, wid), 0) < tile_len[0]
    return jnp.where(live, attended, jnp.bfloat16(0))


def solution(mesh):
    in_specs = (
        P("tile", "head"),
        P("tile", "head"),
        P("tile", "head"),
        P("head"),
        P("head"),
        P("tile", None, "head"),
        P("tile", None, "head"),
        P("tile"),
        P("tile"),
        P("tile", None),
        P("tile"),
    )
    tiles, nh = mesh.shape["tile"], mesh.shape["head"]

    def whole(q, *rest):
        body = functools.partial(per_device, tiles, nh, q.shape[1])
        return jax.shard_map(
            body, mesh=mesh, in_specs=in_specs, out_specs=P("tile", "head"), check_vma=False
        )(q, *rest)

    return whole
```

time: 86.6 us -> 77 us (0.89)
  the two profiles are of different devices: /device:TPU:1 before, /device:TPU:4 now
where the time goes in v2:
time: 77 us; the launch traced here: 76.8 us
  Pallas kernels  72.9 us (95%)
  other arithmetic  1.96 us (3%)
  between operations  1.31 us (2%)
    pallas_call x1, Pallas kernels, per_device(): pl.pallas_call(functools.partial(kernel, tiles, nh, width), out_shape=jax...  72.9 us
    select_n x1, other arithmetic, per_device(): return jnp.where(live, attended, jnp.bfloat16(0))  1.95 us

profile of v2, /device:TPU:4, one launch (start us, length us, event | category | flops | bytes accessed | tf_op | source)
XLA Modules:
  0.0 76.8 jit_solution(13239528756492797322)
XLA Ops:
  1.3 0.6 iota.15.msrc
  1.9 72.9 %tile_attention.1 = bf16[384,640]{1,0:T(8,128)(2,1)} custom-call(s32[2,128]{1,0:T(2,128)} %iota.15.msrc, s32[64]{0:T(128)} %bitcast.6, s32[64]{0:T(128)} %idx_ref.1, f32[640]{0:T(1024)} %gq_hbm.1, f32[640]{0:T(1024)} %gk_hbm.1, bf16[384,640]{1,0:T(8,128)(2,1)} %q_hbm.1, bf16[384,640]{1,0:T(8,128)(2,1)} %k_hbm.1, bf16[384,640]{1,0:T(8,128)(2,1)} %v_hbm.1, ...), custom_call_target="tpu_custom_call" | custom-call | tf_op jit(solution)/shard_map/tile_attention/pallas_call | solution.py:392
  74.9 1.9 %broadcast_select_fusion = bf16[384,640]{1,0:T(8,128)(2,1)} fusion(bf16[384,640]{1,0:T(8,128)(2,1)} %tile_attention.1, pred[384]{0:T(512)(128)(4,1)S(1)} %iota_compare_fusion), kind=kLoop, calls=%fused_computation | loop fusion | flops 245760 | bytes 983424 | tf_op jit(solution)/shard_map/jit(_where)/select_n | solution.py:430
  (2 shorter events, 0.0 us)

commit v3 on v2

--- a/solution.py
+++ b/solution.py
@@ -20,12 +20,12 @@
 
 def kernel(
     tiles, nh, width,
-    msrc, own_ref, idx_ref, gq_hbm, gk_hbm,
+    len_ref, ses_ref, own_hbm, idx_hbm, gq_hbm, gk_hbm,
     q_hbm, k_hbm, v_hbm, mk_hbm, mv_hbm, o_ref,
     kvb, cur_ka, cur_va, cur_kb, cur_vb,
     qr, kr, vr, qn, kn,
-    gq_ref, gk_ref,
-    ssrc, sbuf, shalf, sother, wsrc, wnear, wfar, mrecv, snear, sfar,
+    gq_ref, gk_ref, own_ref, idx_ref,
+    ssrc, sbuf, shalf, sother, wnear, wfar, msrc, mrecv, snear, sfar,
     tail, ekv, sel, far, mkk, mvv,
     acc, mx, ls,
     out_sem, hop_sem, loc, table_sem, near_sem, edge_out, edge_in, tab_loc,
@@ -82,11 +82,11 @@
         pltpu.make_async_copy(a, b, loc.at[i])
         for i, (a, b) in enumerate((
             (q_hbm, qr), (k_hbm, kr), (mk_hbm, kvb.at[0]), (mv_hbm, kvb.at[nz]), (v_hbm, vr),
-            (gq_hbm, gq_ref), (gk_hbm, gk_ref),
+            (gq_hbm, gq_ref), (gk_hbm, gk_ref), (own_hbm, own_ref), (idx_hbm, idx_ref),
         ))
     ]
-    for copy in loads:
-        copy.start()
+    for i in (7, 8, 0, 1, 2, 3, 4, 5, 6):
+        loads[i].start()
 
     lane = lax.broadcasted_iota(jnp.int32, (1, 128), 1)
 
@@ -99,34 +99,34 @@
         )
 
     none = jnp.full((1, 128), -1, jnp.int32)
+    loads[7].wait()
+    loads[8].wait()
     w0, w1 = lax.fori_loop(0, own_ref.shape[0], ask, (none, none))
-    length, session = msrc[0:1, 0:1], msrc[1:2, 0:1]
-    wsrc[0:1, :] = w0
-    wsrc[1:2, :] = w1
+    length, session = len_ref[0], ses_ref[0]
+    wnear[0, 0:1, :] = w0
+    wnear[0, 1:2, :] = w1
+    msrc[0:1, :] = jnp.full((1, 128), length, jnp.int32)
+    msrc[1:2, :] = jnp.full((1, 128), session, jnp.int32)
 
     def tell(rel):
         return pltpu.make_async_remote_copy(
-            src_ref=wsrc, dst_ref=wnear.at[rel], send_sem=out_sem.at[1], recv_sem=table_sem.at[0],
+            src_ref=wnear.at[0], dst_ref=wnear.at[rel], send_sem=out_sem.at[1], recv_sem=table_sem.at[0],
             device_id={"tile": near(rel)}, device_id_type=MESH)
 
-    def tell_far(i, rel):
-        return pltpu.make_async_remote_copy(
-            src_ref=wsrc, dst_ref=wfar.at[(i ^ 1) * 4 + rel], send_sem=out_sem.at[2], recv_sem=table_sem.at[1],
-            device_id={"tile": at(steps[i], rel)}, device_id_type=MESH)
+    def tell_far(i):
+        return pltpu.make_async_remote_copy(
+            src_ref=wnear, dst_ref=wfar.at[pl.ds((i ^ 1) * 4, 4)], send_sem=out_sem.at[2], recv_sem=table_sem.at[1],
+            device_id={"tile": at(steps[i], 0)}, device_id_type=MESH)
 
     def meta(side):
         return pltpu.make_async_remote_copy(
             src_ref=msrc, dst_ref=mrecv.at[side], send_sem=out_sem.at[3], recv_sem=table_sem.at[2],
             device_id={"tile": (right, left)[side]}, device_id_type=MESH)
 
-    wnear[0] = wsrc[...]
     for rel in range(1, 4):
         tell(rel).start()
     meta(0).start()
     meta(1).start()
-    for i in range(4):
-        for rel in range(4):
-            tell_far(i, rel).start()
 
     loads[0].wait()
     loads[1].wait()
@@ -170,6 +170,8 @@
     landed(wnear.at[pl.ds(1, 3)], table_sem.at[0])
     copy = pltpu.make_async_copy(wnear, snear, tab_loc.at[0])
     copy.start()
+    for i in range(4):
+        tell_far(i).start()
     copy.wait()
 
     def edge(side, x):
@@ -236,9 +238,9 @@
     def origin(r):
         return lax.rem(z + nz - r, nz)
 
-    def hand_out(r, x, src):
+    def hand_out(r, x, src, rels=(2, 3, 1, 0)):
         owner = origin(r) * 4 + sub
-        for rel in (2, 3, 1, 0):
+        for rel in rels:
             out = (mkk, mvv)[x].at[r, pl.ds(0, 2)] if rel == 0 else sel.at[(x * 3 + rel - 1) * nz + r]
             for slot in range(2):
                 out[slot] = src[jnp.maximum(snear[rel, slot, owner], 0)]
@@ -248,11 +250,11 @@
                     send_sem=out_sem.at[6], recv_sem=near_sem.at[r],
                     device_id={"tile": near(rel)}, device_id_type=MESH).start()
 
-    def far_out(d, x, src):
+    def far_out(d, x, src, rels):
         owner = origin(full if d == 0 else nz - full) * 4 + sub
-        for far_by in (1, 2) if d == x else (1,):
+        for far_by in (2, 1) if d == x else (1,):
             i, r = (far_by - 1) * 2 + d, (full + far_by) if d == 0 else nz - full - far_by
-            for rel in range(4):
+            for rel in rels:
                 place = (d * 2 + x if far_by == 1 else 4 + d) * 4 + rel
                 for slot in range(2):
                     far[place, slot] = src[jnp.maximum(sfar[i * 4 + rel, slot, owner], 0)]
@@ -325,21 +327,14 @@
     normalise()
     arrived(2, 0)
     take(2, 0)
+    chunk((0,), False, True)
     arrived(2, 1)
     take(2, 1)
     chunk((1, nz - 1), False, True)
-    landed(mrecv, table_sem.at[2])
-    for side, there in ((0, t > 0), (1, t < tiles - 1)):
-
-        @pl.when(there)
-        def _(side=side):
-            landed(ekv.at[side], edge_in.at[side])
-
     @pl.loop(3, full)
     def _(s):
         arrived(s, 0)
         take(s, 0)
-        pl.when(s - 3 < heads)(lambda: own_attention(s - 3))
         arrived(s, 1)
         take(s, 1)
         chunk((s - 1, nz - s + 1), False, True)
@@ -351,13 +346,24 @@
     for x, (up_cur, dn_cur) in enumerate(((cur_ka, cur_kb), (cur_va, cur_vb))):
         hop(0, full, x).wait_recv()
         hop(1, full, x).wait_recv()
-        take(full, x)
-        far_out(0, x, up_cur)
-        far_out(1, x, dn_cur)
+        up_cur[...] = kvb[x * nz + full]
+        dn_cur[...] = kvb[x * nz + nz - full]
+        far_out(0, x, up_cur, (2, 3))
+        far_out(1, x, dn_cur, (2, 3))
+        far_out(0, x, up_cur, (0, 1))
+        far_out(1, x, dn_cur, (0, 1))
+        hand_out(full, x, up_cur)
+        hand_out(nz - full, x, dn_cur)
     chunk((full - 1, nz - full + 1), False, True)
-    for i in range(max(0, full - 3), heads):
+    landed(mrecv, table_sem.at[2])
+    for side, there in ((0, t > 0), (1, t < tiles - 1)):
+
+        @pl.when(there)
+        def _(side=side):
+            landed(ekv.at[side], edge_in.at[side])
+
+    for i in range(heads):
         own_attention(i)
-    chunk((0,), False, True)
     chunk((full, nz - full, half - 1, nz - half + 1, half), True, False)
     for i in range(heads):
         o_ref[:, i * HEAD_DIM : (i + 1) * HEAD_DIM] = (acc[i] / ls[i]).astype(BF16)
@@ -388,11 +394,10 @@
     tile = pltpu.VMEM((cap, wid), BF16)
     state = pltpu.VMEM((heads, cap, HEAD_DIM), F32)
     block = pltpu.VMEM((blocks, rows, wid), BF16)
-    meta = jnp.where(lax.broadcasted_iota(jnp.int32, (2, 128), 0) == 0, tile_len[0], session[0])
     attended = pl.pallas_call(
         functools.partial(kernel, tiles, nh, width),
         out_shape=jax.ShapeDtypeStruct((cap, wid), BF16),
-        in_specs=[vmem] + [smem] * 2 + [hbm] * 7,
+        in_specs=[smem] * 2 + [hbm] * 9,
         out_specs=vmem,
         scratch_shapes=[
             pltpu.VMEM((2 * nz, blocks, rows, wid), BF16),
@@ -400,13 +405,15 @@
             tile, tile, tile, tile, tile,
             pltpu.VMEM((wid,), F32),
             pltpu.VMEM((wid,), F32),
+            pltpu.SMEM(index.shape, jnp.int32),
+            pltpu.SMEM(index.shape, jnp.int32),
             pltpu.VMEM((2, cap), F32),
             pltpu.VMEM((nh // 2, 2, cap), F32),
             pltpu.VMEM((2, cap), F32),
             pltpu.VMEM((2, cap), F32),
-            pltpu.VMEM((2, 128), jnp.int32),
             pltpu.VMEM((4, 2, 128), jnp.int32),
             pltpu.VMEM((16, 2, 128), jnp.int32),
+            pltpu.VMEM((2, 128), jnp.int32),
             pltpu.VMEM((2, 2, 128), jnp.int32),
             pltpu.SMEM((4, 2, 128), jnp.int32),
             pltpu.SMEM((16, 2, 128), jnp.int32),
@@ -417,14 +424,14 @@
             pltpu.VMEM((nz, 8, rows, wid), BF16),
             pltpu.VMEM((nz, 8, rows, wid), BF16),
             state, state, state,
-            sem((8,)), sem((2, half - 2, 2)), sem((7,)), sem((5,)), sem((nz,)), sem((2,)), sem((2,)), sem((2,)),
+            sem((8,)), sem((2, half - 2, 2)), sem((9,)), sem((5,)), sem((nz,)), sem((2,)), sem((2,)), sem((2,)),
         ],
         compiler_params=pltpu.CompilerParams(
-            collective_id=0, has_side_effects=True, vmem_limit_bytes=60 * 1024 * 1024
+            collective_id=0, has_side_effects=True, vmem_limit_bytes=44 * 1024 * 1024
         ),
         name="tile_attention",
     )(
-        meta, owner.reshape(-1), index, gq, gk, q, k, v, mk, mv,
+        tile_len, session, *(pltpu.with_memory_space_constraint(a, pltpu.HBM) for a in (owner.reshape(-1), index, gq, gk, q, k, v, mk, mv)),
     )
     live = lax.broadcasted_iota(jnp.int32, (cap, wid), 0) < tile_len[0]
     return jnp.where(live, attended, jnp.bfloat16(0))

time: 77 us -> 73 us (0.948)
  the two profiles are of different devices: /device:TPU:4 before, /device:TPU:1 now
where the time goes in v3:
time: 73 us; the launch traced here: 71.8 us
  Pallas kernels  69.6 us (95%)
  between operations  1.31 us (2%)
  other arithmetic  0.92 us (1%)
    pallas_call x1, Pallas kernels, per_device(): pl.pallas_call(functools.partial(kernel, tiles, nh, width), out_shape=jax...  69.6 us

profile of v3, /device:TPU:1, one launch (start us, length us, event | category | flops | bytes accessed | tf_op | source)
XLA Modules:
  0.0 71.8 jit_solution(10346089239497846470)
XLA Ops:
  1.3 69.6 %tile_attention.1 = bf16[384,640]{1,0:T(8,128)(2,1)S(1)} custom-call(s32[1]{0:T(128)} %copy.12.len_ref, s32[1]{0:T(128)S(6)} %copy.13.ses_ref, s32[64]{0:T(128)} %bitcast.3, s32[64]{0:T(128)} %idx_hbm.1, f32[640]{0:T(1024)} %gq_hbm.1, f32[640]{0:T(1024)} %gk_hbm.1, bf16[384,640]{1,0:T(8,128)(2,1)} %q_hbm.1, bf16[384,640]{1,0:T(8,128)(2,1)} %k_hbm.1, ...), custom_call_target="tpu_custom_call" | custom-call | tf_op jit(solution)/shard_map/tile_attention/pallas_call | solution.py:397
  70.9 0.9 %broadcast_select_fusion = bf16[384,640]{1,0:T(8,128)(2,1)} fusion(bf16[384,640]{1,0:T(8,128)(2,1)S(1)} %tile_attention.1, pred[384]{0:T(512)(128)(4,1)S(1)} %iota_compare_fusion), kind=kLoop, calls=%fused_computation | loop fusion | flops 245760 | bytes 983424 | tf_op jit(solution)/shard_map/jit(_where)/select_n | solution.py:437
  (1 shorter events, 0.0 us)

commit v4 on v3

--- a/solution.py
+++ b/solution.py
@@ -16,6 +16,7 @@
 BF16 = jnp.bfloat16
 F32 = jnp.float32
 SCORE_SCALE = (1.0 / HEAD_DIM**0.5) * math.log2(math.e)
+LAST_GROUPS = ((0, 1), (2, 3), (4,))
 
 
 def kernel(
@@ -53,8 +54,7 @@
     def at(dz, rel):
         return lax.rem(z + dz + nz, nz) * 4 + near(rel) - z * 4
 
-    greet = [{"tile": near(rel)} for rel in range(1, 4)]
-    greet += [{"tile": at(dz, rel)} for dz in steps for rel in range(4)]
+    greet = [{"tile": up}, {"tile": dn}] + [{"tile": near(rel)} for rel in range(1, 4)]
     greet += [{"head": lax.rem(h + 2 * i, nh)} for i in range(1, nh // 2)]
     hpair = h + jnp.where(lax.rem(h, 2) == 0, 1, -1)
     greet += [{"head": hpair}]
@@ -113,10 +113,12 @@
             src_ref=wnear.at[0], dst_ref=wnear.at[rel], send_sem=out_sem.at[1], recv_sem=table_sem.at[0],
             device_id={"tile": near(rel)}, device_id_type=MESH)
 
-    def tell_far(i):
-        return pltpu.make_async_remote_copy(
-            src_ref=wnear, dst_ref=wfar.at[pl.ds((i ^ 1) * 4, 4)], send_sem=out_sem.at[2], recv_sem=table_sem.at[1],
-            device_id={"tile": at(steps[i], 0)}, device_id_type=MESH)
+    def tell_far(i, far):
+        dst = wfar.at[pl.ds((i ^ 1) * 4 + 8 * far, 4)]
+        return pltpu.make_async_remote_copy(
+            src_ref=wfar.at[pl.ds((i ^ 1) * 4, 4)] if far else wnear, dst_ref=dst,
+            send_sem=out_sem.at[2], recv_sem=table_sem.at[5 if far else 1],
+            device_id={"tile": (up, dn)[i]}, device_id_type=MESH)
 
     def meta(side):
         return pltpu.make_async_remote_copy(
@@ -125,8 +127,6 @@
 
     for rel in range(1, 4):
         tell(rel).start()
-    meta(0).start()
-    meta(1).start()
 
     loads[0].wait()
     loads[1].wait()
@@ -170,8 +170,8 @@
     landed(wnear.at[pl.ds(1, 3)], table_sem.at[0])
     copy = pltpu.make_async_copy(wnear, snear, tab_loc.at[0])
     copy.start()
-    for i in range(4):
-        tell_far(i).start()
+    for i in range(2):
+        tell_far(i, False).start()
     copy.wait()
 
     def edge(side, x):
@@ -288,9 +288,21 @@
 
         if loop:
             pl.loop(0, heads)(one)
-        else:
-            for i in range(heads):
-                one(i)
+            return
+        live = lax.broadcasted_iota(jnp.int32, (cap, HEAD_DIM), 0) < length
+        for some in LAST_GROUPS:
+            cols = [slice(i * HEAD_DIM, (i + 1) * HEAD_DIM) for i in some]
+            scores = [
+                lax.dot_general(qn[:, c], rows(mkk, c), (((1,), (1,)), ((), ())), preferred_element_type=F32)
+                * SCORE_SCALE + bias for c in cols
+            ]
+            now = [jnp.maximum(mx[i], jnp.max(x, axis=1, keepdims=True)) for i, x in zip(some, scores)]
+            expo = [jnp.exp2(x - n[:, :1]) for x, n in zip(scores, now)]
+            keep = [jnp.exp2(mx[i] - n) for i, n in zip(some, now)]
+            whole = [ls[i] * k + jnp.sum(e, axis=1, keepdims=True) for i, k, e in zip(some, keep, expo)]
+            for i, c, k, e, w in zip(some, cols, keep, expo, whole):
+                out = acc[i] * k + jnp.dot(e.astype(BF16), rows(mvv, c), preferred_element_type=F32)
+                o_ref[:, c] = jnp.where(live, out / w, 0.0).astype(BF16)
 
     loads[2].wait()
     loads[3].wait()
@@ -323,6 +335,11 @@
     take(1, 0)
     halves()
     arrived(1, 1)
+    landed(wfar.at[pl.ds(0, 8)], table_sem.at[1])
+    for i in range(2):
+        tell_far(i, True).start()
+    meta(0).start()
+    meta(1).start()
     take(1, 1)
     normalise()
     arrived(2, 0)
@@ -339,7 +356,7 @@
         take(s, 1)
         chunk((s - 1, nz - s + 1), False, True)
 
-    landed(wfar, table_sem.at[1])
+    landed(wfar.at[pl.ds(8, 8)], table_sem.at[5])
     copy = pltpu.make_async_copy(wfar, sfar, tab_loc.at[1])
     copy.start()
     copy.wait()
@@ -365,9 +382,6 @@
     for i in range(heads):
         own_attention(i)
     chunk((full, nz - full, half - 1, nz - half + 1, half), True, False)
-    for i in range(heads):
-        o_ref[:, i * HEAD_DIM : (i + 1) * HEAD_DIM] = (acc[i] / ls[i]).astype(BF16)
-
     landed(kvb.at[pl.ds(0, 4 * full)], out_sem.at[0])
     landed(wnear.at[pl.ds(0, 3)], out_sem.at[1])
     landed(wfar, out_sem.at[2])
@@ -394,7 +408,7 @@
     tile = pltpu.VMEM((cap, wid), BF16)
     state = pltpu.VMEM((heads, cap, HEAD_DIM), F32)
     block = pltpu.VMEM((blocks, rows, wid), BF16)
-    attended = pl.pallas_call(
+    return pl.pallas_call(
         functools.partial(kernel, tiles, nh, width),
         out_shape=jax.ShapeDtypeStruct((cap, wid), BF16),
         in_specs=[smem] * 2 + [hbm] * 9,
@@ -424,7 +438,7 @@
             pltpu.VMEM((nz, 8, rows, wid), BF16),
             pltpu.VMEM((nz, 8, rows, wid), BF16),
             state, state, state,
-            sem((8,)), sem((2, half - 2, 2)), sem((9,)), sem((5,)), sem((nz,)), sem((2,)), sem((2,)), sem((2,)),
+            sem((8,)), sem((2, half - 2, 2)), sem((9,)), sem((6,)), sem((nz,)), sem((2,)), sem((2,)), sem((2,)),
         ],
         compiler_params=pltpu.CompilerParams(
             collective_id=0, has_side_effects=True, vmem_limit_bytes=44 * 1024 * 1024
@@ -433,8 +447,6 @@
     )(
         tile_len, session, *(pltpu.with_memory_space_constraint(a, pltpu.HBM) for a in (owner.reshape(-1), index, gq, gk, q, k, v, mk, mv)),
     )
-    live = lax.broadcasted_iota(jnp.int32, (cap, wid), 0) < tile_len[0]
-    return jnp.where(live, attended, jnp.bfloat16(0))
 
 
 def solution(mesh):

time: 73 us -> 70.3 us (0.963); the launches traced: 71.8 us -> 70.1 us
  Pallas kernels: 69.6 us -> 68 us
  other arithmetic: 0.92 us -> 0 us
  local copies, waits for them, and re-layouts: 0 us -> 0.78 us
    pallas_call x1, Pallas kernels: 69.6 us -> 68 us  [per_device(): pl.pallas_call(functools.partial(kernel, tiles, nh, width), out_shape=jax...]
    select_n x1 -> x0, other arithmetic: 0.92 us -> none  [per_device(): return jnp.where(live, attended, jnp.bfloat16(0))]
    unnamed x0 -> x1, local copies, waits for them, and re-layouts: none -> 0.78 us
where the time goes in v4:
time: 70.3 us; the launch traced here: 70.1 us
  Pallas kernels  68 us (97%)
  between operations  1.3 us (2%)
  local copies, waits for them, and re-layouts  0.78 us (1%)
    pallas_call x1, Pallas kernels, per_device(): pl.pallas_call(functools.partial(kernel, tiles, nh, width), out_shape=jax...  68 us

profile of v4, /device:TPU:1, one launch (start us, length us, event | category | flops | bytes accessed | tf_op | source)
XLA Modules:
  0.0 70.1 jit_solution(9332115199027425974)
XLA Ops:
  1.3 68.0 %tile_attention.1 = bf16[384,640]{1,0:T(8,128)(2,1)S(1)} custom-call(s32[1]{0:T(128)S(6)} %copy.13.len_ref, s32[1]{0:T(128)S(6)} %copy.14.ses_ref, s32[64]{0:T(128)} %bitcast.1, s32[64]{0:T(128)} %idx_hbm.1, f32[640]{0:T(1024)} %gq_hbm.1, f32[640]{0:T(1024)} %gk_hbm.1, bf16[384,640]{1,0:T(8,128)(2,1)} %q_hbm.1, bf16[384,640]{1,0:T(8,128)(2,1)} %k_hbm.1, ...), custom_call_target="tpu_custom_call" | custom-call | tf_op jit(solution)/shard_map/tile_attention/pallas_call | solution.py:411
  69.3 0.8 %copy.15 = bf16[384,640]{1,0:T(8,128)(2,1)} copy(bf16[384,640]{1,0:T(8,128)(2,1)S(1)} %tile_attention.1) | data formatting | bytes 983040

commit v5 on v4

--- a/solution.py
+++ b/solution.py
@@ -60,24 +60,6 @@
     greet += [{"head": hpair}]
     for n in greet:
         pl.semaphore_signal(bar, inc=1, device_id=n, device_id_type=MESH)
-    pl.semaphore_wait(bar, len(greet))
-
-    def hop(d, s, x):
-        first = (mk_hbm, mv_hbm)[x]
-        static = isinstance(s, int)
-        if d == 0:
-            src, dst, dev = s - 1, s, up
-        else:
-            src, dst, dev = nz + 1 - s, nz - s, dn
-        return pltpu.make_async_remote_copy(
-            src_ref=first if static and s == 1 else kvb.at[x * nz + src], dst_ref=kvb.at[x * nz + dst],
-            send_sem=out_sem.at[0], recv_sem=hop_sem.at[d, s - 1, x],
-            device_id={"tile": dev}, device_id_type=MESH)
-
-    for x in range(2):
-        for d in range(2):
-            hop(d, 1, x).start()
-
     loads = [
         pltpu.make_async_copy(a, b, loc.at[i])
         for i, (a, b) in enumerate((
@@ -85,8 +67,24 @@
             (gq_hbm, gq_ref), (gk_hbm, gk_ref), (own_hbm, own_ref), (idx_hbm, idx_ref),
         ))
     ]
-    for i in (7, 8, 0, 1, 2, 3, 4, 5, 6):
+    for i in (2, 3, 7, 8, 0, 1, 4, 5, 6):
         loads[i].start()
+    pl.semaphore_wait(bar, len(greet))
+
+    def hop(d, s, x):
+        if d == 0:
+            src, dst, dev = s - 1, s, up
+        else:
+            src, dst, dev = 0 if isinstance(s, int) and s == 1 else nz + 1 - s, nz - s, dn
+        return pltpu.make_async_remote_copy(
+            src_ref=kvb.at[x * nz + src], dst_ref=kvb.at[x * nz + dst],
+            send_sem=out_sem.at[0], recv_sem=hop_sem.at[d, s - 1, x],
+            device_id={"tile": dev}, device_id_type=MESH)
+
+    for x in range(2):
+        loads[2 + x].wait()
+        for d in range(2):
+            hop(d, 1, x).start()
 
     lane = lax.broadcasted_iota(jnp.int32, (1, 128), 1)
 
@@ -207,13 +205,17 @@
             for x in range(2):
                 edge(1, x).start()
 
+    def spread(x, width):
+        parts = [x] * (width // HEAD_DIM) + ([x[:, : width % HEAD_DIM]] if width % HEAD_DIM else [])
+        return parts[0] if len(parts) == 1 else jnp.concatenate(parts, 1)
+
     def update(i, keys, values, bias):
         cols = pl.ds(pl.multiple_of(i * HEAD_DIM, HEAD_DIM), HEAD_DIM)
         scores = lax.dot_general(qn[:, cols], keys(cols), (((1,), (1,)), ((), ())), preferred_element_type=F32)
         scores = scores * SCORE_SCALE + bias
         before = mx[i]
         now = jnp.maximum(before, jnp.max(scores, axis=1, keepdims=True))
-        expo = jnp.exp2(scores - now[:, :1])
+        expo = jnp.exp2(scores - spread(now, scores.shape[1]))
         keep = jnp.exp2(before - now)
         mx[i] = now
         ls[i] = ls[i] * keep + jnp.sum(expo, axis=1, keepdims=True)
@@ -297,15 +299,13 @@
                 * SCORE_SCALE + bias for c in cols
             ]
             now = [jnp.maximum(mx[i], jnp.max(x, axis=1, keepdims=True)) for i, x in zip(some, scores)]
-            expo = [jnp.exp2(x - n[:, :1]) for x, n in zip(scores, now)]
+            expo = [jnp.exp2(x - spread(n, x.shape[1])) for x, n in zip(scores, now)]
             keep = [jnp.exp2(mx[i] - n) for i, n in zip(some, now)]
             whole = [ls[i] * k + jnp.sum(e, axis=1, keepdims=True) for i, k, e in zip(some, keep, expo)]
             for i, c, k, e, w in zip(some, cols, keep, expo, whole):
                 out = acc[i] * k + jnp.dot(e.astype(BF16), rows(mvv, c), preferred_element_type=F32)
                 o_ref[:, c] = jnp.where(live, out / w, 0.0).astype(BF16)
 
-    loads[2].wait()
-    loads[3].wait()
     cur_ka[...] = kvb[0]
     cur_va[...] = kvb[nz]
     hand_out(0, 0, cur_ka)
@@ -341,10 +341,9 @@
     meta(0).start()
     meta(1).start()
     take(1, 1)
-    normalise()
     arrived(2, 0)
     take(2, 0)
-    chunk((0,), False, True)
+    normalise()
     arrived(2, 1)
     take(2, 1)
     chunk((1, nz - 1), False, True)
@@ -352,6 +351,7 @@
     def _(s):
         arrived(s, 0)
         take(s, 0)
+        pl.when(s == 3)(lambda: chunk((0,), False, True))
         arrived(s, 1)
         take(s, 1)
         chunk((s - 1, nz - s + 1), False, True)

time: 70.3 us -> 69.4 us (0.987)
  Pallas kernels: 68 us -> 67.2 us
    pallas_call x1, Pallas kernels: 68 us -> 67.2 us  [per_device(): pl.pallas_call(functools.partial(kernel, tiles, nh, width), out_shape=jax...]
where the time goes in v5:
time: 69.4 us; the launch traced here: 69.3 us
  Pallas kernels  67.2 us (97%)
  between operations  1.3 us (2%)
  local copies, waits for them, and re-layouts  0.78 us (1%)
    pallas_call x1, Pallas kernels, per_device(): pl.pallas_call(functools.partial(kernel, tiles, nh, width), out_shape=jax...  67.2 us

profile of v5, /device:TPU:1, one launch (start us, length us, event | category | flops | bytes accessed | tf_op | source)
XLA Modules:
  0.0 69.3 jit_solution(3737332400953648096)
XLA Ops:
  1.3 67.2 %tile_attention.1 = bf16[384,640]{1,0:T(8,128)(2,1)S(1)} custom-call(s32[1]{0:T(128)S(6)} %copy.13.len_ref, s32[1]{0:T(128)S(6)} %copy.14.ses_ref, s32[64]{0:T(128)} %bitcast.1, s32[64]{0:T(128)} %idx_hbm.1, f32[640]{0:T(1024)} %gq_hbm.1, f32[640]{0:T(1024)} %gk_hbm.1, bf16[384,640]{1,0:T(8,128)(2,1)} %q_hbm.1, bf16[384,640]{1,0:T(8,128)(2,1)} %k_hbm.1, ...), custom_call_target="tpu_custom_call" | custom-call | tf_op jit(solution)/shard_map/tile_attention/pallas_call | solution.py:411
  68.5 0.8 %copy.15 = bf16[384,640]{1,0:T(8,128)(2,1)} copy(bf16[384,640]{1,0:T(8,128)(2,1)S(1)} %tile_attention.1) | data formatting | bytes 983040

commit v6 on v5

--- a/solution.py
+++ b/solution.py
@@ -16,7 +16,7 @@
 BF16 = jnp.bfloat16
 F32 = jnp.float32
 SCORE_SCALE = (1.0 / HEAD_DIM**0.5) * math.log2(math.e)
-LAST_GROUPS = ((0, 1), (2, 3), (4,))
+LAST_GROUPS = ((0, 1, 2), (3, 4))
 
 
 def kernel(

time: 69.4 us -> 69.3 us (level)
  no operation moved by 1% of the time
where the time goes in v6:
time: 69.3 us; the launch traced here: 69.1 us
  Pallas kernels  67.1 us (97%)
  between operations  1.3 us (2%)
  local copies, waits for them, and re-layouts  0.78 us (1%)
    pallas_call x1, Pallas kernels, per_device(): pl.pallas_call(functools.partial(kernel, tiles, nh, width), out_shape=jax...  67.1 us

profile of v6, /device:TPU:1, one launch (start us, length us, event | category | flops | bytes accessed | tf_op | source)
XLA Modules:
  0.0 69.1 jit_solution(15099119278554682980)
XLA Ops:
  1.3 67.1 %tile_attention.1 = bf16[384,640]{1,0:T(8,128)(2,1)S(1)} custom-call(s32[1]{0:T(128)S(6)} %copy.13.len_ref, s32[1]{0:T(128)S(6)} %copy.14.ses_ref, s32[64]{0:T(128)} %bitcast.1, s32[64]{0:T(128)} %idx_hbm.1, f32[640]{0:T(1024)} %gq_hbm.1, f32[640]{0:T(1024)} %gk_hbm.1, bf16[384,640]{1,0:T(8,128)(2,1)} %q_hbm.1, bf16[384,640]{1,0:T(8,128)(2,1)} %k_hbm.1, ...), custom_call_target="tpu_custom_call" | custom-call | tf_op jit(solution)/shard_map/tile_attention/pallas_call | solution.py:411
  68.4 0.8 %copy.15 = bf16[384,640]{1,0:T(8,128)(2,1)} copy(bf16[384,640]{1,0:T(8,128)(2,1)S(1)} %tile_attention.1) | data formatting | bytes 983040
